TPU v7x, 256 devices: a whole 4x4x8 slice. The times are simulated.
256 devices in a mesh: dp: 32 (over x, z), mp: 8 (over y, core).
Axes of the slice: x: 4, y: 4, z: 8, core: 2. Of those that a mesh axis runs over, the one named last changes fastest.
Arguments:
- grad_parts: bfloat16 [32, 16, 1024, 1024], P('dp', None, None, 'mp'), may hold values from -6 to 6
- owners: int32 [16], replicated, may hold values from 0 to 7, as said below
- left_stat: float32 [32, 1024, 1024], P('mp', 'dp'), may hold values from -1 to 8
- right_stat: float32 [32, 1024, 1024], P('mp', 'dp'), may hold values from -1 to 8
- left_root: bfloat16 [32, 1024, 1024], P('mp', 'dp'), may hold values from -1 to 9
- right_root: bfloat16 [32, 1024, 1024], P('mp'), may hold values from -1 to 3
- first_moment: float32 [32, 1024, 1024], P('mp', 'dp'), may hold values from -32 to 32
- second_moment: float32 [32, 1024, 1024], P('mp', 'dp'), may hold values from 0.5 to 2
- vec_grad: bfloat16 [32, 73728], P('dp', 'mp'), may hold values from -3 to 3
- vec_first: float32 [73728], P('mp'), may hold values from -4 to 4
- vec_second: float32 [73728], P('mp'), may hold values from 0.5 to 2
Outputs:
- block_update: bfloat16 [16, 1024, 1024], P(None, 'dp', 'mp')
- left_new: float32 [32, 1024, 1024], P('mp', 'dp')
- right_new: float32 [32, 1024, 1024], P('mp', 'dp')
- first_new: float32 [32, 1024, 1024], P('mp', 'dp')
- second_new: float32 [32, 1024, 1024], P('mp', 'dp')
- vec_update: bfloat16 [73728], P('mp')
- vec_first_new: float32 [73728], P('mp')
- vec_second_new: float32 [73728], P('mp')
Inputs may be any that keep to these rules, and one draw needn't show every extreme that they name: `owners`: no owner holds more than 4 blocks, and in every draw some owner holds exactly 4.
All inputs are finite; a program needn't handle non-finite values.
Results may differ from a plain program's by a relative error of at most 0.018.
Values may be sent and summed in bfloat16 or wider, within the bound.
A program may use at most 128 MiB of HBM per device.

v0:
```python
import jax
import jax.numpy as jnp
from jax import lax
from jax.sharding import PartitionSpec as P

beta_one = 0.9
beta_two = 0.95
adam_eps = 1e-08
graft_eps = 1e-06


def owner_table(owners, owner_count, slot_count):
    block_count = owners.shape[0]
    same = owners[:, None] == owners[None, :]
    earlier = lax.broadcasted_iota(jnp.int32, (block_count, block_count), 1) < lax.broadcasted_iota(
        jnp.int32, (block_count, block_count), 0
    )
    slots = jnp.sum((same & earlier).astype(jnp.int32), axis=1)
    owner_ids = lax.broadcasted_iota(jnp.int32, (owner_count, slot_count, block_count), 0)
    slot_ids = lax.broadcasted_iota(jnp.int32, (owner_count, slot_count, block_count), 1)
    return ((owners[None, None, :] == owner_ids) & (slots[None, None, :] == slot_ids)).astype(
        jnp.float32
    )


def body(
    grad_parts,
    owners,
    left_stat,
    right_stat,
    left_root,
    right_root,
    first_moment,
    second_moment,
    vec_grad,
    vec_first,
    vec_second,
):
    owner_count = lax.axis_size("mp")
    slot_count, row_count, order = left_stat.shape
    col_count = order // owner_count
    my_rows = lax.axis_index("dp") * row_count
    my_owner = lax.axis_index("mp")
    row_pieces = lax.psum_scatter(
        grad_parts[0].astype(jnp.float32).astype(jnp.bfloat16),
        "dp",
        scatter_dimension=1,
        tiled=True,
    ).astype(jnp.float32)
    selector = owner_table(owners, owner_count, slot_count)
    outgoing = jnp.einsum("ocb,brw->crow", selector, row_pieces, precision=lax.Precision.HIGHEST)
    incoming = lax.all_to_all(
        outgoing.astype(jnp.bfloat16), "mp", split_axis=2, concat_axis=2, tiled=True
    ).astype(outgoing.dtype)
    grad_rows = incoming.reshape(slot_count, row_count, order)
    mine = lax.dynamic_index_in_dim(selector, my_owner, 0, keepdims=False)
    used_mask = (jnp.sum(mine, axis=1) > 0.5)[:, None, None]
    rounded_rows = grad_rows.astype(jnp.bfloat16)
    shard_rows = lax.all_gather(rounded_rows, "dp", axis=1, tiled=True)
    left_part = jnp.einsum(
        "crk,cnk->crn", rounded_rows, shard_rows, preferred_element_type=jnp.float32
    )
    own_cols = lax.dynamic_slice_in_dim(shard_rows, my_rows, row_count, 2)
    right_acc = jnp.einsum("cnr,cnk->crk", own_cols, shard_rows, preferred_element_type=jnp.float32)
    applied_acc = jnp.einsum(
        "crn,cnk->crk", left_root, shard_rows, preferred_element_type=jnp.float32
    )
    scale = 1.0 / order
    left_new = jnp.where(used_mask, left_stat + left_part * scale, left_stat)
    right_new = jnp.where(used_mask, right_stat + right_acc * scale, right_stat)
    first_new = jnp.where(
        used_mask, beta_one * first_moment + (1.0 - beta_one) * grad_rows, first_moment
    )
    second_new = jnp.where(
        used_mask,
        beta_two * second_moment + (1.0 - beta_two) * grad_rows * grad_rows,
        second_moment,
    )
    adam = first_new / (jnp.sqrt(second_new) + adam_eps)
    precond = jnp.einsum(
        "crk,ckm->crm",
        applied_acc.astype(jnp.bfloat16),
        right_root,
        preferred_element_type=jnp.float32,
    )
    square_adam = jnp.sum(adam * adam, axis=(1, 2))
    square_pre = jnp.sum(precond * precond, axis=(1, 2))
    squares = lax.all_gather(jnp.stack([square_adam, square_pre]), "dp")
    square_adam, square_pre = jnp.sum(squares, axis=0)
    vec_all = lax.all_gather(vec_grad[0], "dp")
    vec_sum = jnp.sum(vec_all.astype(jnp.float32), axis=0)
    cells = float(order * order)
    graft = jnp.sqrt(square_adam / cells) / jnp.sqrt(square_pre / cells + graft_eps)
    update_rows = (precond * graft[:, None, None]).astype(jnp.bfloat16)
    returned = lax.all_to_all(
        update_rows.reshape(slot_count, row_count, owner_count, col_count),
        "mp",
        split_axis=2,
        concat_axis=2,
        tiled=True,
    )
    block_update = jnp.einsum(
        "ocb,crow->brw", selector.astype(jnp.bfloat16), returned, preferred_element_type=jnp.float32
    ).astype(jnp.bfloat16)
    vec_first_new = beta_one * vec_first + (1.0 - beta_one) * vec_sum
    vec_second_new = beta_two * vec_second + (1.0 - beta_two) * vec_sum * vec_sum
    vec_update = (vec_first_new / (jnp.sqrt(vec_second_new) + adam_eps)).astype(jnp.bfloat16)
    return (
        block_update,
        left_new,
        right_new,
        first_new,
        second_new,
        vec_update,
        vec_first_new,
        vec_second_new,
    )


def solution(mesh):
    placed = (
        P("dp", None, None, "mp"),
        P(),
        P("mp", "dp", None),
        P("mp", "dp", None),
        P("mp", "dp", None),
        P("mp", None, None),
        P("mp", "dp", None),
        P("mp", "dp", None),
        P("dp", "mp"),
        P("mp"),
        P("mp"),
    )
    return jax.shard_map(
        body,
        mesh=mesh,
        in_specs=placed,
        out_specs=(
            P(None, "dp", "mp"),
            P("mp", "dp", None),
            P("mp", "dp", None),
            P("mp", "dp", None),
            P("mp", "dp", None),
            P("mp"),
            P("mp"),
            P("mp"),
        ),
        check_vma=False,
    )
```

profile of v0, /device:TPU:1, one launch (start us, length us, event | category | flops | bytes accessed | tf_op | source)
XLA Modules:
  0.0 420.2 jit_solution(11740701285527777204)
XLA Ops:
  7.2 0.0 copy-start
  7.2 0.0 copy-start.6
  7.2 0.0 copy-start.7
  7.2 0.0 copy-start.3
  7.2 0.0 copy-start.4
  7.2 0.0 reduce-scatter.2.cloned.1.call-start
  7.3 0.7 reduce-scatter.2.cloned.1.call-update
  8.0 0.0 all-gather.5.cloned.1.call-start
  8.0 0.9 convert_reduce_fusion.1
  8.9 223.8 %reduce-scatter.2.cloned.1.call-done = bf16[16,32,128]{2,1,0:T(8,128)(2,1)} async-done(((bf16[16,1024,128]{2,1,0:T(8,128)(2,1)}), bf16[16,32,128]{2,1,0:T(8,128)(2,1)}) %reduce-scatter.2.cloned.1.call-update) | async-done | bytes 131088 | tf_op jit(solution)/shard_map/reduce_scatter | solution.py:44
  232.8 1.1 fusion.4
  233.9 16.5 %all_to_all.10 = bf16[4,32,8,128]{3,1,0,2:T(8,128)(2,1)S(1)} all-to-all(bf16[4,32,8,128]{3,1,0,2:T(8,128)(2,1)S(1)} %copy.31), channel_id=1, replica_groups=mesh['dp'=32,'mp'=8] {'mp'}, dimensions={2} | all-to-all | bytes 524288 | tf_op jit(solution)/shard_map/all_to_all | solution.py:52
  250.4 0.7 copy_bitcast_fusion
  251.2 0.0 all-gather.5.cloned.1.call-update
  251.2 0.7 fusion.19
  251.9 0.1 dynamic-slice_reduce_fusion
  252.0 39.8 %all-gather.2 = bf16[32,1,9216]{2,1,0:T(2,128)(2,1)S(1)} all-gather(bf16[1,1,9216]{2,1,0:T(2,128)(2,1)} %bitcast.55), channel_id=1, replica_groups=mesh['dp'=32,'mp'=8] {'dp'}, dimensions={0}, use_global_device_ids=true | all-gather | bytes 608256 | tf_op jit(solution)/shard_map/all_gather | solution.py:90
  291.8 1.3 convert_reduce_fusion
  293.1 0.0 copy-done.6
  293.1 0.0 copy-done.7
  293.1 0.6 divide_convert_fusion
  293.8 0.0 copy-done.3
  293.8 0.0 copy-done.4
  293.8 1.4 multiply_reduce_fusion.1
  295.2 0.0 copy-start.2
  295.2 51.2 %all-gather.5.cloned.1.call-done = bf16[4,1024,1024]{2,1,0:T(8,128)(2,1)} async-done(((bf16[4,32,1024]{2,1,0:T(8,128)(2,1)}), bf16[4,1024,1024]{2,1,0:T(8,128)(2,1)}) %all-gather.5.cloned.1.call-update) | async-done | bytes 8388624 | tf_op jit(solution)/shard_map/all_gather | solution.py:59
  346.4 0.0 copy-done
  346.4 8.9 %multiply_reduce_fusion = (f32[4]{0:T(128)S(1)}, f32[4,32,1024]{2,1,0:T(8,128)S(1)}) fusion(bf16[4,1024,1024]{2,1,0:T(8,128)(2,1)} %param.16, bf16[4,32,1024]{2,1,0:T(8,128)(2,1)S(1)} %copy-done, bf16[4,1024,1024]{2,1,0:T(8,128)(2,1)} %all-gather.5.cloned.1.call-done), kind=kOutput, calls=%fused_computation.21 | convolution fusion | flops 537264128 | bytes 17563664 | tf_op jit(solution)/shard_map/crk,ckm->crm/dot_general | solution.py:80
  355.2 0.0 copy-start.5
  355.2 31.0 %all-gather.1 = f32[32,2,4]{2,1,0:T(2,128)S(1)} all-gather(f32[1,2,4]{2,1,0:T(2,128)S(1)} %maximum_bitcast_fusion), channel_id=2, replica_groups=mesh['dp'=32,'mp'=8] {'dp'}, dimensions={0}, use_global_device_ids=true | all-gather | bytes 1056 | tf_op jit(solution)/shard_map/all_gather | solution.py:88
  386.3 0.1 multiply_convert_fusion
  386.5 0.9 copy.33
  387.4 15.5 %all-to-all-start.1 = ((bf16[4,32,8,128]{3,0,1,2:T(4,128)(2,1)}), bf16[4,32,8,128]{3,0,1,2:T(4,128)(2,1)S(1)}, u32[]{:S(2)}, u32[]{:S(2)}) async-start(bf16[4,32,8,128]{3,0,1,2:T(4,128)(2,1)} %copy.33), calls=%async_computation.2 | async-start | bytes 524288 | tf_op jit(solution)/shard_map/all_to_all | solution.py:95
  402.8 0.0 copy-done.2
  402.9 0.0 copy-start.1
  402.9 0.0 copy-start.8
  402.9 6.9 %fusion.1 = f32[4,32,1024]{2,1,0:T(8,128)} fusion(f32[4,32,1024]{2,1,0:T(8,128)S(1)} %copy-done.2, bf16[4,1024,1024]{2,1,0:T(8,128)(2,1)} %all-gather.5.cloned.1.call-done, pred[4]{0:T(512)(128)(4,1)S(1)} %broadcast_compare_fusion, bf16[4,32,8,128]{3,1,0,2:T(8,128)(2,1)S(1)} %all_to_all.10), kind=kOutput, calls=%fused_computation.3 | convolution fusion | flops 268828672 | bytes 9699332 | tf_op jit(solution)/shard_map/crk,cnk->crn/dot_general | solution.py:60
  409.8 0.0 copy-done.5
  409.8 0.0 copy-done.1
  409.8 2.6 fusion.3
  412.4 0.0 all-to-all-done.1
  412.4 0.0 copy-done.8
  412.4 0.3 fusion.5
  412.7 0.7 copy.36
  (6 shorter events, 0.2 us)
Async XLA Ops:
  7.2 339.2 %copy-start = (bf16[4,32,1024]{2,1,0:T(8,128)(2,1)S(1)}, bf16[4,32,1024]{2,1,0:T(8,128)(2,1)}, u32[]{:S(2)}) copy-start(bf16[4,32,1024]{2,1,0:T(8,128)(2,1)} %param.15) | copy-start | bytes 786436
  7.2 285.9 %copy-start.6 = (f32[9216]{0:T(1024)S(1)}, f32[9216]{0:T(1024)}, u32[]{:S(2)}) copy-start(f32[9216]{0:T(1024)} %param.21) | copy-start | bytes 110596
  7.2 285.9 %copy-start.7 = (f32[9216]{0:T(1024)S(1)}, f32[9216]{0:T(1024)}, u32[]{:S(2)}) copy-start(f32[9216]{0:T(1024)} %param.20) | copy-start | bytes 110596
  7.2 286.6 %copy-start.3 = (f32[4,32,1024]{2,1,0:T(8,128)S(1)}, f32[4,32,1024]{2,1,0:T(8,128)}, u32[]{:S(2)}) copy-start(f32[4,32,1024]{2,1,0:T(8,128)} %param.18) | copy-start | bytes 1572868
  7.2 286.6 %copy-start.4 = (f32[4,32,1024]{2,1,0:T(8,128)S(1)}, f32[4,32,1024]{2,1,0:T(8,128)}, u32[]{:S(2)}) copy-start(f32[4,32,1024]{2,1,0:T(8,128)} %param.17) | copy-start | bytes 1572868
  7.2 225.5 %reduce-scatter.2.cloned.1.call-start = ((), (), s32[]{:S(2)}) async-start(), calls=%async_computation.3 | async-start | bytes 4325376 | tf_op jit(solution)/shard_map/reduce_scatter | solution.py:44
  8.0 338.4 %all-gather.5.cloned.1.call-start = ((), (), s32[]{:S(2)}) async-start(), calls=%async_computation.4 | async-start | bytes 8650752 | tf_op jit(solution)/shard_map/all_gather | solution.py:59
  295.2 107.7 %copy-start.2 = (f32[4,32,1024]{2,1,0:T(8,128)S(1)}, f32[4,32,1024]{2,1,0:T(8,128)}, u32[]{:S(2)}) copy-start(f32[4,32,1024]{2,1,0:T(8,128)} %param.13) | copy-start | bytes 1572868
  355.2 54.6 %copy-start.5 = (f32[4,32,1024]{2,1,0:T(8,128)S(1)}, f32[4,32,1024]{2,1,0:T(8,128)}, u32[]{:S(2)}) copy-start(f32[4,32,1024]{2,1,0:T(8,128)} %param.14) | copy-start | bytes 1572868
  387.4 25.0 %all-to-all-start.1 = ((bf16[4,32,8,128]{3,0,1,2:T(4,128)(2,1)}), bf16[4,32,8,128]{3,0,1,2:T(4,128)(2,1)S(1)}, u32[]{:S(2)}, u32[]{:S(2)}) async-start(bf16[4,32,8,128]{3,0,1,2:T(4,128)(2,1)} %copy.33), calls=%async_computation.2 | async-start | bytes 524288 | tf_op jit(solution)/shard_map/all_to_all | solution.py:95
  402.9 6.9 %copy-start.1 = (bf16[4,1024,1024]{2,1,0:T(8,128)(2,1)S(1)}, bf16[4,1024,1024]{2,1,0:T(8,128)(2,1)}, u32[]{:S(2)}) copy-start(bf16[4,1024,1024]{2,1,0:T(8,128)(2,1)} %all-gather.5.cloned.1.call-done) | copy-start | bytes 25165828
  402.9 9.6 %copy-start.8 = (s32[16]{0:T(128)S(1)}, s32[16]{0:T(128)}, u32[]{:S(2)}) copy-start(s32[16]{0:T(128)} %param.12) | copy-start | bytes 196
Sparse Core Ops, SparseCore 0:
  12.0 220.7 reduce-scatter.1
  251.3 94.9 all-gather.4
where the time goes:
time: 421 us; the launch traced here: 420 us
  waiting for transfers between devices  276 us (66%)
  blocking collectives  87.3 us (21%)
  matrix products  19.8 us (5%)
  starting transfers between devices  15.5 us (4%)
  between operations  14.2 us (3%)
  other arithmetic  5.23 us (1%)
    reduce_scatter x1, waiting for transfers between devices, body(): lax.psum_scatter(grad_parts[0].astype(jnp.float32).astype(jnp.bfloat16),...  224 us
    all_gather x1, waiting for transfers between devices, body(): shard_rows = lax.all_gather(rounded_rows, 'dp', axis=1, tiled=True)  51.2 us
    all_gather x1, blocking collectives, body(): vec_all = lax.all_gather(vec_grad[0], 'dp')  39.8 us
    all_gather x1, blocking collectives, body(): squares = lax.all_gather(jnp.stack([square_adam, square_pre]), 'dp')  31 us
    all_to_all x1, blocking collectives, body(): lax.all_to_all(outgoing.astype(jnp.bfloat16), 'mp', split_axis=2, concat_...  16.5 us
    all_to_all x1, starting transfers between devices, body(): lax.all_to_all(update_rows.reshape(slot_count, row_count, owner_count, co...  15.5 us
    dot_general x1, matrix products, body(): jnp.einsum('crk,ckm->crm', applied_acc.astype(jnp.bfloat16), right_root,...  8.86 us
  transfers between devices with their start and end apart: 3, of which 2 were waited for; matrix products, arithmetic and copies ran while one was open for 3% of the time, Pallas kernels for 0%

commit v1 on v0

--- a/solution.py
+++ b/solution.py
@@ -56,7 +56,15 @@
     mine = lax.dynamic_index_in_dim(selector, my_owner, 0, keepdims=False)
     used_mask = (jnp.sum(mine, axis=1) > 0.5)[:, None, None]
     rounded_rows = grad_rows.astype(jnp.bfloat16)
-    shard_rows = lax.all_gather(rounded_rows, "dp", axis=1, tiled=True)
+    shard_rows = jnp.concatenate(
+        jax.lax.all_to_all(
+            jnp.stack([rounded_rows] * jax.lax.axis_size("dp"), axis=0),
+            axis_name="dp",
+            split_axis=0,
+            concat_axis=0,
+        ),
+        axis=1,
+    )
     left_part = jnp.einsum(
         "crk,cnk->crn", rounded_rows, shard_rows, preferred_element_type=jnp.float32
     )

time: 421 us -> 585 us (1.39)
  blocking collectives: 87.3 us -> 267 us
  waiting for transfers between devices: 276 us -> 225 us
  starting transfers between devices: 15.5 us -> 39.9 us
  local copies, waits for them, and re-layouts: 2.48 us -> 14.5 us
    all_gather x1, blocking collectives: 39.8 us -> 220 us  [body(): vec_all = lax.all_gather(vec_grad[0], 'dp')]
    all_gather x1 -> x0, waiting for transfers between devices: 51.2 us -> none  [body(): shard_rows = lax.all_gather(rounded_rows, 'dp', axis=1, tiled=True)]
    all_to_all x1, starting transfers between devices: 15.5 us -> 33.2 us  [body(): lax.all_to_all(update_rows.reshape(slot_count, row_count, owner_count, co...]
    reshape x0 -> x1, local copies, waits for them, and re-layouts: none -> 8.46 us  [body(): jnp.concatenate(jax.lax.all_to_all(jnp.stack([rounded_rows] * jax.lax.axi...]
    all_to_all x0 -> x1, starting transfers between devices: none -> 6.62 us  [body(): jax.lax.all_to_all(jnp.stack([rounded_rows] * jax.lax.axis_size('dp'), ax...]
  transfers between devices with their start and end apart: 3 -> 3, of which waited for: 2 -> 1; matrix products, arithmetic and copies ran while one was open for 3% -> 2% of each run, Pallas kernels for 0% -> 0%
where the time goes in v1:
time: 585 us
  blocking collectives  267 us (46%)
  waiting for transfers between devices  225 us (38%)
  starting transfers between devices  39.9 us (7%)
  matrix products  19.9 us (3%)
  local copies, waits for them, and re-layouts  14.5 us (2%)
  between operations  14.2 us (2%)
    reduce_scatter x1, waiting for transfers between devices, body(): lax.psum_scatter(grad_parts[0].astype(jnp.float32).astype(jnp.bfloat16),...  224 us
    all_gather x1, blocking collectives, body(): vec_all = lax.all_gather(vec_grad[0], 'dp')  220 us
    all_to_all x1, starting transfers between devices, body(): lax.all_to_all(update_rows.reshape(slot_count, row_count, owner_count, co...  33.2 us
    all_gather x1, blocking collectives, body(): squares = lax.all_gather(jnp.stack([square_adam, square_pre]), 'dp')  30.7 us
    all_to_all x1, blocking collectives, body(): lax.all_to_all(outgoing.astype(jnp.bfloat16), 'mp', split_axis=2, concat_...  16.5 us
  transfers between devices with their start and end apart: 3, of which 1 were waited for; matrix products, arithmetic and copies ran while one was open for 2% of the time, Pallas kernels for 0%

profile of v1, /device:TPU:1, one launch (start us, length us, event | category | flops | bytes accessed | tf_op | source)
XLA Modules:
  0.0 584.9 jit_solution(10811623409406870568)
XLA Ops:
  7.2 0.0 copy-start
  7.2 0.0 reduce-scatter.2.cloned.1.call-start
  7.2 0.7 reduce-scatter.2.cloned.1.call-update
  7.9 0.9 convert_reduce_fusion.1
  8.8 223.9 %reduce-scatter.2.cloned.1.call-done = bf16[16,32,128]{2,1,0:T(8,128)(2,1)} async-done(((bf16[16,1024,128]{2,1,0:T(8,128)(2,1)}), bf16[16,32,128]{2,1,0:T(8,128)(2,1)}) %reduce-scatter.2.cloned.1.call-update) | async-done | bytes 131088 | tf_op jit(solution)/shard_map/reduce_scatter | solution.py:44
  232.7 1.1 fusion.4
  233.9 16.5 %all_to_all.15 = bf16[4,32,8,128]{3,1,0,2:T(8,128)(2,1)S(1)} all-to-all(bf16[4,32,8,128]{3,1,0,2:T(8,128)(2,1)S(1)} %copy.32), channel_id=1, replica_groups=mesh['dp'=32,'mp'=8] {'mp'}, dimensions={2} | all-to-all | bytes 524288 | tf_op jit(solution)/shard_map/all_to_all | solution.py:52
  250.4 4.3 stack.8
  254.7 0.0 copy-start.9
  254.7 0.0 copy-start.6
  254.7 0.0 copy-start.7
  254.7 0.0 copy-start.8
  254.7 0.0 copy-start.3
  254.7 0.0 copy-start.4
  254.8 6.6 %all-to-all-start.1 = ((bf16[32,4,32,1024]{3,2,1,0:T(8,128)(2,1)}), bf16[32,4,32,1024]{3,2,1,0:T(8,128)(2,1)}, u32[]{:S(2)}, u32[]{:S(2)}) async-start(bf16[32,4,32,1024]{3,2,1,0:T(8,128)(2,1)} %stack.8), calls=%async_computation.2 | async-start | bytes 16777216 | tf_op jit(solution)/shard_map/all_to_all | solution.py:60
  261.4 0.0 copy-done.9
  261.4 0.1 dynamic-slice_reduce_fusion
  261.5 0.0 copy-done.6
  261.5 220.2 %all-gather.2 = bf16[32,1,9216]{2,1,0:T(2,128)(2,1)S(1)} all-gather(bf16[1,1,9216]{2,1,0:T(2,128)(2,1)S(1)} %bitcast.60), channel_id=1, replica_groups=mesh['dp'=32,'mp'=8] {'dp'}, dimensions={0}, use_global_device_ids=true | all-gather | bytes 608256 | tf_op jit(solution)/shard_map/all_gather | solution.py:98
  481.7 1.3 convert_reduce_fusion
  483.1 0.0 copy-done.7
  483.1 0.0 copy-done.8
  483.1 0.6 divide_convert_fusion
  483.7 0.0 copy-done.3
  483.7 0.0 copy-done.4
  483.7 1.4 multiply_reduce_fusion.1
  485.1 0.0 all-to-all-done.1
  485.1 8.5 %copy.34 = bf16[4,32,32,1024]{3,2,1,0:T(8,128)(2,1)} copy(bf16[4,32,32,1024]{3,2,0,1:T(8,128)(2,1)} %bitcast.6) | data formatting | bytes 16777216 | tf_op jit(solution)/shard_map/reshape | solution.py:59
  493.6 0.0 copy-done
  493.6 0.0 copy-start.2
  493.6 8.9 %multiply_reduce_fusion = (f32[4]{0:T(128)S(1)}, f32[4,32,1024]{2,1,0:T(8,128)S(1)}) fusion(bf16[4,1024,1024]{2,1,0:T(8,128)(2,1)} %param.16, bf16[4,32,1024]{2,1,0:T(8,128)(2,1)S(1)} %copy-done, bf16[4,1024,1024]{2,1,0:T(8,128)(2,1)} %bitcast.54), kind=kOutput, calls=%fused_computation.21 | convolution fusion | flops 537264128 | bytes 17563664 | tf_op jit(solution)/shard_map/crk,ckm->crm/dot_general | solution.py:88
  502.5 0.0 copy-start.5
  502.5 30.7 %all-gather.1 = f32[32,2,4]{2,1,0:T(2,128)S(1)} all-gather(f32[1,2,4]{2,1,0:T(2,128)S(1)} %maximum_bitcast_fusion), channel_id=2, replica_groups=mesh['dp'=32,'mp'=8] {'dp'}, dimensions={0}, use_global_device_ids=true | all-gather | bytes 1056 | tf_op jit(solution)/shard_map/all_gather | solution.py:96
  533.2 0.1 multiply_convert_fusion
  533.4 0.9 copy.35
  534.3 33.2 %all-to-all-start.2 = ((bf16[4,32,8,128]{3,0,1,2:T(4,128)(2,1)}), bf16[4,32,8,128]{3,0,1,2:T(4,128)(2,1)S(1)}, u32[]{:S(2)}, u32[]{:S(2)}) async-start(bf16[4,32,8,128]{3,0,1,2:T(4,128)(2,1)} %copy.35), calls=%async_computation.3 | async-start | bytes 524288 | tf_op jit(solution)/shard_map/all_to_all | solution.py:103
  567.5 0.0 copy-done.2
  567.5 0.0 copy-start.1
  567.5 6.9 %fusion.1 = f32[4,32,1024]{2,1,0:T(8,128)} fusion(f32[4,32,1024]{2,1,0:T(8,128)S(1)} %copy-done.2, bf16[4,1024,1024]{2,1,0:T(8,128)(2,1)} %bitcast.55, pred[4]{0:T(512)(128)(4,1)S(1)} %broadcast_compare_fusion, bf16[4,32,8,128]{3,1,0,2:T(8,128)(2,1)S(1)} %all_to_all.15), kind=kOutput, calls=%fused_computation.3 | convolution fusion | flops 268828672 | bytes 9699332 | tf_op jit(solution)/shard_map/crk,cnk->crn/dot_general | solution.py:68
  574.4 0.0 copy-done.5
  574.4 0.0 copy-done.1
  574.4 2.6 fusion.3
  577.0 0.0 all-to-all-done.2
  577.0 0.3 fusion.5
  577.3 0.7 copy.38
  (8 shorter events, 0.2 us)
Async XLA Ops:
  7.2 486.4 %copy-start = (bf16[4,32,1024]{2,1,0:T(8,128)(2,1)S(1)}, bf16[4,32,1024]{2,1,0:T(8,128)(2,1)}, u32[]{:S(2)}) copy-start(bf16[4,32,1024]{2,1,0:T(8,128)(2,1)} %param.15) | copy-start | bytes 786436
  7.2 225.5 %reduce-scatter.2.cloned.1.call-start = ((), (), s32[]{:S(2)}) async-start(), calls=%async_computation.4 | async-start | bytes 4325376 | tf_op jit(solution)/shard_map/reduce_scatter | solution.py:44
  254.7 6.7 %copy-start.9 = (s32[16]{0:T(128)S(1)}, s32[16]{0:T(128)}, u32[]{:S(2)}) copy-start(s32[16]{0:T(128)} %param.12) | copy-start | bytes 196
  254.7 6.8 %copy-start.6 = (bf16[1,9216]{1,0:T(2,128)(2,1)S(1)}, bf16[1,9216]{1,0:T(2,128)(2,1)}, u32[]{:S(2)}) copy-start(bf16[1,9216]{1,0:T(2,128)(2,1)} %param.19) | copy-start | bytes 55300
  254.7 228.3 %copy-start.7 = (f32[9216]{0:T(1024)S(1)}, f32[9216]{0:T(1024)}, u32[]{:S(2)}) copy-start(f32[9216]{0:T(1024)} %param.21) | copy-start | bytes 110596
  254.7 228.3 %copy-start.8 = (f32[9216]{0:T(1024)S(1)}, f32[9216]{0:T(1024)}, u32[]{:S(2)}) copy-start(f32[9216]{0:T(1024)} %param.20) | copy-start | bytes 110596
  254.7 229.0 %copy-start.3 = (f32[4,32,1024]{2,1,0:T(8,128)S(1)}, f32[4,32,1024]{2,1,0:T(8,128)}, u32[]{:S(2)}) copy-start(f32[4,32,1024]{2,1,0:T(8,128)} %param.18) | copy-start | bytes 1572868
  254.7 229.0 %copy-start.4 = (f32[4,32,1024]{2,1,0:T(8,128)S(1)}, f32[4,32,1024]{2,1,0:T(8,128)}, u32[]{:S(2)}) copy-start(f32[4,32,1024]{2,1,0:T(8,128)} %param.17) | copy-start | bytes 1572868
  254.8 230.3 %all-to-all-start.1 = ((bf16[32,4,32,1024]{3,2,1,0:T(8,128)(2,1)}), bf16[32,4,32,1024]{3,2,1,0:T(8,128)(2,1)}, u32[]{:S(2)}, u32[]{:S(2)}) async-start(bf16[32,4,32,1024]{3,2,1,0:T(8,128)(2,1)} %stack.8), calls=%async_computation.2 | async-start | bytes 16777216 | tf_op jit(solution)/shard_map/all_to_all | solution.py:60
  493.6 73.9 %copy-start.2 = (f32[4,32,1024]{2,1,0:T(8,128)S(1)}, f32[4,32,1024]{2,1,0:T(8,128)}, u32[]{:S(2)}) copy-start(f32[4,32,1024]{2,1,0:T(8,128)} %param.13) | copy-start | bytes 1572868
  502.5 71.9 %copy-start.5 = (f32[4,32,1024]{2,1,0:T(8,128)S(1)}, f32[4,32,1024]{2,1,0:T(8,128)}, u32[]{:S(2)}) copy-start(f32[4,32,1024]{2,1,0:T(8,128)} %param.14) | copy-start | bytes 1572868
  534.3 42.8 %all-to-all-start.2 = ((bf16[4,32,8,128]{3,0,1,2:T(4,128)(2,1)}), bf16[4,32,8,128]{3,0,1,2:T(4,128)(2,1)S(1)}, u32[]{:S(2)}, u32[]{:S(2)}) async-start(bf16[4,32,8,128]{3,0,1,2:T(4,128)(2,1)} %copy.35), calls=%async_computation.3 | async-start | bytes 524288 | tf_op jit(solution)/shard_map/all_to_all | solution.py:103
  567.5 6.9 %copy-start.1 = (bf16[4,32,32,1024]{3,2,1,0:T(8,128)(2,1)S(1)}, bf16[4,32,32,1024]{3,2,1,0:T(8,128)(2,1)}, u32[]{:S(2)}) copy-start(bf16[4,32,32,1024]{3,2,1,0:T(8,128)(2,1)} %copy.34) | copy-start | bytes 25165828
Sparse Core Ops, SparseCore 0:
  11.9 220.7 reduce-scatter.1
